TPU v7x, 32 devices: a whole 2x2x4 slice. The times are simulated.
32 devices in a mesh: batch: 4 (over x, core), lat: 4 (over z), lon: 2 (over y).
Axes of the slice: x: 2, y: 2, z: 4, core: 2. Of those that a mesh axis runs over, the one named last changes fastest.
Arguments:
- tokens: bfloat16 [4, 2, 48, 48, 1024], P('batch', None, 'lat', 'lon'), may hold values from -6 to 6
- weights: bfloat16 [1024, 4096], P('batch')
- regions: int32 [2, 48, 48], P(None, 'lat', 'lon'), may hold values from 0 to 3
- offsets: int32 [2], replicated, may hold values from 1 to 11, as said below
Outputs:
- mixed: bfloat16 [4, 2, 48, 48, 1024], P('batch', None, 'lat', 'lon')
Inputs may be any that keep to these rules, and one draw needn't show every extreme that they name: `offsets`: element 0 lies from 1 to 5; element 1 equals 11.
All inputs are finite; a program needn't handle non-finite values.
Results may differ from a plain program's by a relative error of at most 0.0042.
Values may be sent and summed in bfloat16 or wider, within the bound.
A program may use at most 128 MiB of HBM per device.

v0:
```python
import jax
import jax.numpy as jnp
from jax import lax
from jax.sharding import PartitionSpec as P

HEADS = 16
WLEV = 2
WLAT = 6
WLON = 12


def from_behind(block, axis, distance):
    devices = range(lax.axis_size(axis))
    route = [((i - distance) % len(devices), i) for i in devices]
    return lax.ppermute(block, axis, route)


def layer_norm(field):
    field = field.astype(jnp.float32)
    average = jnp.mean(field, -1, keepdims=True)
    centred = field - average
    variance = jnp.mean(centred * centred, -1, keepdims=True)
    return (centred * lax.rsqrt(variance + 1e-05)).astype(jnp.bfloat16)


def windows(field):
    levels, rows_lat, cols_lon, features = field.shape
    field = field.reshape(
        levels // WLEV, WLEV, rows_lat // WLAT, WLAT, cols_lon // WLON, WLON, features
    )
    field = field.transpose(0, 2, 4, 1, 3, 5, 6)
    return field.reshape(-1, WLEV * WLAT * WLON, features)


def unwindows(field, levels, rows_lat, cols_lon):
    features = field.shape[-1]
    field = field.reshape(
        levels // WLEV, rows_lat // WLAT, cols_lon // WLON, WLEV, WLAT, WLON, features
    )
    field = field.transpose(0, 3, 1, 4, 2, 5, 6)
    return field.reshape(levels, rows_lat, cols_lon, features)


def attend(normed, all_weights, regions):
    levels, rows_lat, cols_lon, width = normed.shape
    qkv = jnp.dot(
        normed.reshape(-1, width), all_weights[:, : 3 * width], preferred_element_type=jnp.float32
    ).astype(jnp.bfloat16)
    qkv = windows(qkv.reshape(levels, rows_lat, cols_lon, 3 * width))
    num_windows, win_size = (qkv.shape[0], qkv.shape[1])
    head_size = width // HEADS
    queries = qkv[..., :width].reshape(num_windows, win_size, HEADS, head_size)
    keys_all = qkv[..., width : 2 * width].reshape(num_windows, win_size, HEADS, head_size)
    values_all = qkv[..., 2 * width :].reshape(num_windows, win_size, HEADS, head_size)
    scores = jnp.einsum(
        "wqhe,wkhe->whqk", queries, keys_all, preferred_element_type=jnp.float32
    ) * head_size ** (-0.5)
    region_ids = windows(regions[..., None])[..., 0]
    allowed = region_ids[:, None, :, None] == region_ids[:, None, None, :]
    scores = jnp.where(allowed, scores, -1e30)
    largest = jnp.max(scores, -1, keepdims=True)
    expsc = jnp.exp(scores - largest)
    attn_probs = (expsc / jnp.sum(expsc, -1, keepdims=True)).astype(jnp.bfloat16)
    mixed_out = jnp.einsum(
        "whqk,wkhe->wqhe", attn_probs, values_all, preferred_element_type=jnp.float32
    )
    mixed_out = mixed_out.astype(jnp.bfloat16).reshape(num_windows, win_size, width)
    return unwindows(mixed_out, levels, rows_lat, cols_lon)


def roll_forward(block_in, offsets):
    rows_lat, cols_lon = (block_in.shape[1], block_in.shape[2])
    from_next = from_behind(block_in[:, :WLAT], "lat", -1)
    joined = jnp.concatenate([block_in, from_next], axis=1)
    block_in = lax.dynamic_slice_in_dim(joined, offsets[0], rows_lat, 1)
    from_next = from_behind(block_in[:, :, :WLON], "lon", -1)
    joined = jnp.concatenate([block_in, from_next], axis=2)
    return lax.dynamic_slice_in_dim(joined, offsets[1], cols_lon, 2)


def roll_back(block_in, offsets):
    rows_lat, cols_lon = (block_in.shape[1], block_in.shape[2])
    from_prev = from_behind(block_in[:, rows_lat - WLAT :], "lat", 1)
    joined = jnp.concatenate([from_prev, block_in], axis=1)
    block_in = lax.dynamic_slice_in_dim(joined, WLAT - offsets[0], rows_lat, 1)
    from_prev = from_behind(block_in[:, :, cols_lon - WLON :], "lon", 1)
    joined = jnp.concatenate([from_prev, block_in], axis=2)
    return lax.dynamic_slice_in_dim(joined, WLON - offsets[1], cols_lon, 2)


def local(tokens, weights, regions, offsets):
    width = weights.shape[1] // 4
    all_weights = lax.all_gather(weights, "batch", axis=0, tiled=True)
    block_in = tokens[0]
    rolled = roll_forward(block_in, offsets)
    attended = attend(layer_norm(rolled), all_weights, regions)
    back_rolled = roll_back(attended, offsets)
    projected = jnp.dot(
        back_rolled.reshape(-1, width),
        all_weights[:, 3 * width :],
        preferred_element_type=jnp.float32,
    )
    mixed = block_in.astype(jnp.float32) + projected.reshape(block_in.shape)
    return mixed.astype(jnp.bfloat16)[None]


def solution(mesh):
    in_specs = (P("batch", None, "lat", "lon", None), P("batch", None), P(None, "lat", "lon"), P())
    out_specs = P("batch", None, "lat", "lon", None)
    return jax.shard_map(local, mesh=mesh, in_specs=in_specs, out_specs=out_specs, check_vma=False)
```

profile of v0, /device:TPU:0, one launch (start us, length us, event | category | flops | bytes accessed | tf_op | source)
XLA Modules:
  0.0 174.3 jit_solution(2364879644640626707)
XLA Ops:
  6.5 0.7 all-gather.2.cloned.1.call-update
  7.3 0.5 copy-done.2
  7.8 5.1 %collective-permute-start = (bf16[2,6,24,1024]{3,2,1,0:T(8,128)(2,1)S(1)}, bf16[2,6,24,1024]{3,2,1,0:T(8,128)(2,1)S(1)}, u32[]{:S(2)}, u32[]{:S(2)}) collective-permute-start(bf16[2,6,24,1024]{3,2,1,0:T(8,128)(2,1)S(1)} %slice.46), channel_id=1, source_target_pairs={{2,0},{4,2},{6,4},{0,6},{3,1},{5,3},{7,5},{1,7},{10,8},{12,10},{14... | collective-permute-start | bytes 1769480 | tf_op jit(solution)/shard_map/ppermute | solution.py:15
  13.0 0.6 fusion.30
  15.6 9.9 %collective-permute-done = bf16[2,6,24,1024]{3,2,1,0:T(8,128)(2,1)S(1)} collective-permute-done((bf16[2,6,24,1024]{3,2,1,0:T(8,128)(2,1)S(1)}, bf16[2,6,24,1024]{3,2,1,0:T(8,128)(2,1)S(1)}, u32[]{:S(2)}, u32[]{:S(2)}) %collective-permute-start) | collective-permute-done | bytes 589856 | tf_op jit(solution)/shard_map/ppermute | solution.py:15
  26.0 0.6 copy.17
  26.6 1.6 collective-permute-start.1
  30.1 0.8 broadcast_compare_fusion
  30.9 9.9 %collective-permute-done.1 = bf16[2,12,12,1024]{3,0,2,1:T(2,128)(2,1)S(1)} collective-permute-done((bf16[2,12,12,1024]{3,0,2,1:T(2,128)(2,1)S(1)}, bf16[2,12,12,1024]{3,0,2,1:T(2,128)(2,1)S(1)}, u32[]{:S(2)}, u32[]{:S(2)}) %collective-permute-start.1) | collective-permute-done | bytes 589856 | tf_op jit(solution)/shard_map/ppermute | solution.py:15
  41.0 1.1 convert_reduce_fusion
  42.1 0.4 fusion.13
  42.5 1.4 fusion.14
  43.9 26.1 %all-gather.2.cloned.1.call-done = bf16[1024,4096]{1,0:T(8,128)(2,1)} async-done(((bf16[256,4096]{1,0:T(8,128)(2,1)}), bf16[1024,4096]{1,0:T(8,128)(2,1)}) %all-gather.2.cloned.1.call-update) | async-done | bytes 8388624 | tf_op jit(solution)/shard_map/all_gather | solution.py:93
  69.9 7.0 %fusion.8 = bf16[576,3072]{1,0:T(8,128)(2,1)S(1)} fusion(bf16[576,1024]{1,0:T(8,128)(2,1)} %bitcast.51, bf16[1024,4096]{1,0:T(8,128)(2,1)} %all-gather.2.cloned.1.call-done), kind=kOutput, calls=%fused_computation.11 | convolution fusion | flops 3625648128 | bytes 11010048 | tf_op jit(solution)/shard_map/dot_general | solution.py:46
  76.9 3.5 %reshape_reshape.6 = bf16[1,2,2,6,2,12,3072]{6,5,4,3,2,1,0:T(8,128)(2,1)} reshape(bf16[576,3072]{1,0:T(8,128)(2,1)S(1)} %fusion.8) | data formatting | bytes 7077888 | tf_op jit(solution)/shard_map/reshape;reshape | solution.py:28
  80.5 7.8 %copy.19 = bf16[1,2,2,2,6,12,3072]{6,2,1,5,4,3,0:T(2,128)(2,1)} copy(bf16[1,2,2,2,6,12,3072]{6,5,2,4,1,3,0:T(8,128)(2,1)} %bitcast.43) | data formatting | bytes 7077888 | tf_op jit(solution)/shard_map/transpose | solution.py:31
  88.2 7.7 %reshape.45 = bf16[4,144,3072]{2,0,1:T(4,128)(2,1)S(1)} reshape(bf16[1,2,2,2,6,12,3072]{6,2,1,5,4,3,0:T(2,128)(2,1)} %copy.19) | data formatting | bytes 7077888 | tf_op jit(solution)/shard_map/reshape | solution.py:32
  95.9 2.7 %fusion.29 = (bf16[4,144,1024]{2,0,1:T(4,128)(2,1)}, bf16[4,144,1024]{2,0,1:T(4,128)(2,1)}, bf16[4,144,1024]{2,0,1:T(4,128)(2,1)}) fusion(bf16[4,144,3072]{2,0,1:T(4,128)(2,1)S(1)} %reshape.45), kind=kLoop, calls=%fused_computation.44 | loop fusion | bytes 7077888 | tf_op jit(solution)/shard_map/slice | solution.py:53
  98.6 4.1 %copy.22 = bf16[4,144,1024]{1,2,0:T(8,128)(2,1)} copy(bf16[4,144,1024]{2,0,1:T(4,128)(2,1)} %get-tuple-element.8) | data formatting | bytes 2359296 | tf_op jit(solution)/shard_map/slice | solution.py:52
  102.7 2.5 %copy.23 = bf16[4,144,1024]{1,2,0:T(8,128)(2,1)} copy(bf16[4,144,1024]{2,0,1:T(4,128)(2,1)S(1)} %copy-done.1) | data formatting | bytes 2359296 | tf_op jit(solution)/shard_map/slice | solution.py:53
  105.1 2.5 %copy.20 = bf16[4,144,1024]{1,2,0:T(8,128)(2,1)} copy(bf16[4,144,1024]{2,0,1:T(4,128)(2,1)S(1)} %copy-done) | data formatting | bytes 2359296 | tf_op jit(solution)/shard_map/slice | solution.py:54
  107.6 8.8 %fusion.31 = (f32[4,16,144]{2,1,0:T(8,128)S(1)}, f32[4,16,144,144]{2,3,1,0:T(8,128)}) fusion(pred[4,144,144]{1,2,0:T(8,128)(4,1)S(1)} %copy-done.5, bf16[4,144,16,64]{1,3,2,0:T(8,128)(2,1)S(1)} %bitcast.48, bf16[4,144,16,64]{1,3,2,0:T(8,128)(2,1)} %bitcast.49), kind=kOutput, calls=%fused_computation.46 | convolution fusion | flops 175177872 | bytes 7787520 | tf_op jit(solution)/shard_map/sub | solution.py:62
  116.4 6.5 %convert_bitcast_fusion = bf16[4,144,16,64]{1,3,2,0:T(8,128)(2,1)} fusion(bf16[4,144,16,64]{1,3,2,0:T(8,128)(2,1)} %bitcast.50, f32[4,16,144,144]{2,3,1,0:T(8,128)} %get-tuple-element.13, f32[4,16,144]{2,1,0:T(8,128)S(1)} %get-tuple-element.12), kind=kOutput, calls=%fused_computation.21 | convolution fusion | flops 173113344 | bytes 7704576 | tf_op jit(solution)/shard_map/whqk,wkhe->wqhe/dot_general | solution.py:64
  123.0 3.8 %copy.25 = bf16[4,144,16,64]{3,2,0,1:T(8,128)(2,1)S(1)} copy(bf16[4,144,16,64]{1,3,2,0:T(8,128)(2,1)} %convert_bitcast_fusion) | data formatting | bytes 2359296 | tf_op jit(solution)/shard_map/convert_element_type | solution.py:67
  126.8 1.4 reshape_reshape.7
  128.2 1.2 copy.26
  129.8 1.5 collective-permute-start.2
  132.7 14.4 %collective-permute-done.2 = bf16[2,6,24,1024]{3,2,1,0:T(8,128)(2,1)S(1)} collective-permute-done((bf16[2,6,24,1024]{3,2,1,0:T(8,128)(2,1)S(1)}, bf16[2,6,24,1024]{3,2,1,0:T(8,128)(2,1)S(1)}, u32[]{:S(2)}, u32[]{:S(2)}) %collective-permute-start.2) | collective-permute-done | bytes 589856 | tf_op jit(solution)/shard_map/ppermute | solution.py:15
  147.6 0.6 copy.29
  148.2 1.5 collective-permute-start.3
  150.9 12.1 %collective-permute-done.3 = bf16[2,12,12,1024]{3,0,2,1:T(2,128)(2,1)S(1)} collective-permute-done((bf16[2,12,12,1024]{3,0,2,1:T(2,128)(2,1)S(1)}, bf16[2,12,12,1024]{3,0,2,1:T(2,128)(2,1)S(1)}, u32[]{:S(2)}, u32[]{:S(2)}) %collective-permute-start.3) | collective-permute-done | bytes 589856 | tf_op jit(solution)/shard_map/ppermute | solution.py:15
  163.2 4.3 %fusion.16 = bf16[1,2,12,24,1024]{4,3,2,1,0:T(8,128)(2,1)} fusion(bf16[1024,4096]{1,0:T(8,128)(2,1)} %all-gather.2.cloned.1.call-done, s32[]{:T(128)S(6)} %select_n.20, bf16[2,12,12,1024]{3,2,1,0:T(8,128)(2,1)S(1)} %copy.30, bf16[2,12,24,1024]{3,2,1,0:T(8,128)(2,1)S(1)} %fusion.17, bf16[1,2,12,24,1024]{4,3,2,1,0:T(8,128)(2,1)S(1)} %copy-done.3), kind=kOutput, calls=%fused_computation.30 | convolution fusion | flops 1212088320 | bytes 6225924 | tf_op jit(solution)/shard_map/dot_general | solution.py:98
  (30 shorter events, 1.8 us)
Async XLA Ops:
  6.5 1.3 copy-start.2
  6.5 6.4 %copy-start.7 = (s32[2]{0:T(128)S(1)}, s32[2]{0:T(128)}, u32[]{:S(2)}) copy-start(s32[2]{0:T(128)} %param.7) | copy-start | bytes 28
  6.5 63.4 %all-gather.2.cloned.1.call-start = ((), (), s32[]{:S(2)}) async-start(), calls=%async_computation | async-start | bytes 10485760 | tf_op jit(solution)/shard_map/all_gather | solution.py:93
  7.8 17.7 %collective-permute-start = (bf16[2,6,24,1024]{3,2,1,0:T(8,128)(2,1)S(1)}, bf16[2,6,24,1024]{3,2,1,0:T(8,128)(2,1)S(1)}, u32[]{:S(2)}, u32[]{:S(2)}) collective-permute-start(bf16[2,6,24,1024]{3,2,1,0:T(8,128)(2,1)S(1)} %slice.46), channel_id=1, source_target_pairs={{2,0},{4,2},{6,4},{0,6},{3,1},{5,3},{7,5},{1,7},{10,8},{12,10},{14... | collective-permute-start | bytes 1769480 | tf_op jit(solution)/shard_map/ppermute | solution.py:15
  25.9 3.4 %copy-start.6 = (s32[2,12,24]{2,0,1:T(2,128)S(1)}, s32[2,12,24]{2,0,1:T(2,128)}, u32[]{:S(2)}) copy-start(s32[2,12,24]{2,0,1:T(2,128)} %param.6) | copy-start | bytes 6916
  26.6 14.3 %collective-permute-start.1 = (bf16[2,12,12,1024]{3,0,2,1:T(2,128)(2,1)S(1)}, bf16[2,12,12,1024]{3,0,2,1:T(2,128)(2,1)S(1)}, u32[]{:S(2)}, u32[]{:S(2)}) collective-permute-start(bf16[2,12,12,1024]{3,0,2,1:T(2,128)(2,1)S(1)} %copy.17), channel_id=1, source_target_pairs={{1,0},{0,1},{3,2},{2,3},{5,4},{4,5},{7,6},{6,7},{9,8},{8,9},{11,10... | collective-permute-start | bytes 1769480 | tf_op jit(solution)/shard_map/ppermute | solution.py:15
  98.6 4.1 %copy-start.1 = (bf16[4,144,1024]{2,0,1:T(4,128)(2,1)S(1)}, bf16[4,144,1024]{2,0,1:T(4,128)(2,1)}, u32[]{:S(2)}) copy-start(bf16[4,144,1024]{2,0,1:T(4,128)(2,1)} %get-tuple-element.7) | copy-start | bytes 3538948
  102.7 2.5 %copy-start = (bf16[4,144,1024]{2,0,1:T(4,128)(2,1)S(1)}, bf16[4,144,1024]{2,0,1:T(4,128)(2,1)}, u32[]{:S(2)}) copy-start(bf16[4,144,1024]{2,0,1:T(4,128)(2,1)} %get-tuple-element.9) | copy-start | bytes 3538948
  105.1 2.5 %copy-start.4 = (bf16[4,144,1024]{1,2,0:T(8,128)(2,1)S(1)}, bf16[4,144,1024]{1,2,0:T(8,128)(2,1)}, u32[]{:S(2)}) copy-start(bf16[4,144,1024]{1,2,0:T(8,128)(2,1)} %copy.22) | copy-start | bytes 3538948
  105.1 2.5 %copy-start.5 = (pred[4,144,144]{1,2,0:T(8,128)(4,1)S(1)}, pred[4,144,144]{1,2,0:T(8,128)(4,1)}, u32[]{:S(2)}) copy-start(pred[4,144,144]{1,2,0:T(8,128)(4,1)} %broadcast_compare_fusion) | copy-start | bytes 248836
  129.8 17.3 %collective-permute-start.2 = (bf16[2,6,24,1024]{3,2,1,0:T(8,128)(2,1)S(1)}, bf16[2,6,24,1024]{3,2,1,0:T(8,128)(2,1)S(1)}, u32[]{:S(2)}, u32[]{:S(2)}) collective-permute-start(bf16[2,6,24,1024]{3,2,1,0:T(8,128)(2,1)S(1)} %slice.52), channel_id=1, source_target_pairs={{6,0},{0,2},{2,4},{4,6},{7,1},{1,3},{3,5},{5,7},{14,8},{8,10},{10,... | collective-permute-start | bytes 1769480 | tf_op jit(solution)/shard_map/ppermute | solution.py:15
  147.4 15.8 %copy-start.3 = (bf16[1,2,12,24,1024]{4,3,2,1,0:T(8,128)(2,1)S(1)}, bf16[1,2,12,24,1024]{4,3,2,1,0:T(8,128)(2,1)}, u32[]{:S(2)}) copy-start(bf16[1,2,12,24,1024]{4,3,2,1,0:T(8,128)(2,1)} %param.4) | copy-start | bytes 3538948
  148.2 14.8 %collective-permute-start.3 = (bf16[2,12,12,1024]{3,0,2,1:T(2,128)(2,1)S(1)}, bf16[2,12,12,1024]{3,0,2,1:T(2,128)(2,1)S(1)}, u32[]{:S(2)}, u32[]{:S(2)}) collective-permute-start(bf16[2,12,12,1024]{3,0,2,1:T(2,128)(2,1)S(1)} %copy.29), channel_id=1, source_target_pairs={{1,0},{0,1},{3,2},{2,3},{5,4},{4,5},{7,6},{6,7},{9,8},{8,9},{11,10... | collective-permute-start | bytes 1769480 | tf_op jit(solution)/shard_map/ppermute | solution.py:15
Sparse Core Ops, SparseCore 0:
  8.9 60.9 all-gather.1
where the time goes:
time: 175 us; the launch traced here: 174 us
  waiting for transfers between devices  73.1 us (42%)
  local copies, waits for them, and re-layouts  40.6 us (23%)
  matrix products  26.7 us (15%)
  between operations  19.9 us (11%)
  starting transfers between devices  9.77 us (6%)
  other arithmetic  4.29 us (2%)
    ppermute x4, waiting for transfers between devices, from_behind(): return lax.ppermute(block, axis, route)  46.3 us
    all_gather x1, waiting for transfers between devices, local(): all_weights = lax.all_gather(weights, 'batch', axis=0, tiled=True)  26.1 us
    ppermute x4, starting transfers between devices, from_behind(): return lax.ppermute(block, axis, route)  9.77 us
    sub x1, matrix products, attend(): expsc = jnp.exp(scores - largest)  8.82 us
    transpose x1, local copies, waits for them, and re-layouts, windows(): field = field.transpose(0, 2, 4, 1, 3, 5, 6)  7.79 us
    reshape x1, local copies, waits for them, and re-layouts, windows(): return field.reshape(-1, WLEV * WLAT * WLON, features)  7.66 us
    dot_general x1, matrix products, attend(): jnp.dot(normed.reshape(-1, width), all_weights[:, :3 * width], preferred_...  6.98 us
    dot_general x1, matrix products, attend(): jnp.einsum('whqk,wkhe->wqhe', attn_probs, values_all, preferred_element_t...  6.52 us
  transfers between devices with their start and end apart: 5, of which 5 were waited for; matrix products, arithmetic and copies ran while one was open for 3% of the time, Pallas kernels for 0%

commit v1 on v0

--- a/solution.py
+++ b/solution.py
@@ -7,6 +7,12 @@
 WLEV = 2
 WLAT = 6
 WLON = 12
+
+
+def in_order(tiles, dim):
+    shape = list(tiles.shape[1:])
+    shape[dim] *= tiles.shape[0]
+    return jnp.moveaxis(tiles, 0, dim).reshape(shape)
 
 
 def from_behind(block, axis, distance):
@@ -90,7 +96,19 @@
 
 def local(tokens, weights, regions, offsets):
     width = weights.shape[1] // 4
-    all_weights = lax.all_gather(weights, "batch", axis=0, tiled=True)
+    devices_2 = lax.axis_size("batch")
+    pairs = [(i_2, (i_2 + 1) % devices_2) for i_2 in range(devices_2)]
+    back = [(b, a) for a, b in pairs]
+    lower, upper = ([], [])
+    for turn in range(devices_2 - 1):
+        if turn % 2 == 0:
+            lower.append(lax.ppermute(lower[-1] if lower else weights, "batch", pairs))
+        else:
+            upper.append(lax.ppermute(upper[-1] if upper else weights, "batch", back))
+    blocks = jnp.stack([*lower[::-1], weights, *upper])
+    shift = lax.axis_index("batch") - len(lower)
+    blocks = blocks[(jnp.arange(devices_2) - shift) % devices_2]
+    all_weights = in_order(blocks, 0)
     block_in = tokens[0]
     rolled = roll_forward(block_in, offsets)
     attended = attend(layer_norm(rolled), all_weights, regions)

time: 175 us -> 196 us (1.12)
  local copies, waits for them, and re-layouts: 40.6 us -> 57.4 us
  between operations: 19.9 us -> 6.13 us
  other arithmetic: 4.29 us -> 16.7 us
  starting transfers between devices: 9.77 us -> 14.4 us
    ppermute x0 -> x3, waiting for transfers between devices: none -> 36.6 us  [the longest x2 36.6 us: local(): lower.append(lax.ppermute(lower[-1] if lower else weights, 'batch', pairs))]
    all_gather x1 -> x0, waiting for transfers between devices: 26.1 us -> none  [local(): all_weights = lax.all_gather(weights, 'batch', axis=0, tiled=True)]
    gather x0 -> x3, local copies, waits for them, and re-layouts: none -> 13.8 us  [local(): blocks = blocks[(jnp.arange(devices_2) - shift) % devices_2]]
    ppermute x4, waiting for transfers between devices: 46.3 us -> 37.5 us  [from_behind(): return lax.ppermute(block, axis, route)]
    unnamed x0 -> x1, other arithmetic: none -> 7.86 us
    ppermute x0 -> x3, starting transfers between devices: none -> 3.73 us  [the longest x2 2.26 us: local(): lower.append(lax.ppermute(lower[-1] if lower else weights, 'batch', pairs))]
    another operation x0 -> x1, other arithmetic: none -> 3.33 us  [local(): blocks = jnp.stack([*lower[::-1], weights, *upper])]
  transfers between devices with their start and end apart: 5 -> 7, of which waited for: 5 -> 5; matrix products, arithmetic and copies ran while one was open for 3% -> 5% of each run, Pallas kernels for 0% -> 0%
where the time goes in v1:
time: 196 us; the launch traced here: 195 us
  waiting for transfers between devices  74.1 us (38%)
  local copies, waits for them, and re-layouts  57.4 us (29%)
  matrix products  26.7 us (14%)
  other arithmetic  16.7 us (9%)
  starting transfers between devices  14.4 us (7%)
  between operations  6.13 us (3%)
    ppermute x4, waiting for transfers between devices, from_behind(): return lax.ppermute(block, axis, route)  37.5 us
    ppermute x2, waiting for transfers between devices, local(): lower.append(lax.ppermute(lower[-1] if lower else weights, 'batch', pairs))  36.6 us
    gather x3, local copies, waits for them, and re-layouts, local(): blocks = blocks[(jnp.arange(devices_2) - shift) % devices_2]  13.8 us
    ppermute x4, starting transfers between devices, from_behind(): return lax.ppermute(block, axis, route)  10.7 us
    sub x1, matrix products, attend(): expsc = jnp.exp(scores - largest)  8.83 us
    unnamed x1, other arithmetic  7.86 us
    transpose x1, local copies, waits for them, and re-layouts, windows(): field = field.transpose(0, 2, 4, 1, 3, 5, 6)  7.79 us
    reshape x1, local copies, waits for them, and re-layouts, windows(): return field.reshape(-1, WLEV * WLAT * WLON, features)  7.66 us
  transfers between devices with their start and end apart: 7, of which 5 were waited for; matrix products, arithmetic and copies ran while one was open for 5% of the time, Pallas kernels for 0%

profile of v1, /device:TPU:0, one launch (start us, length us, event | category | flops | bytes accessed | tf_op | source)
XLA Modules:
  0.0 195.5 jit_solution(5786486419297205219)
XLA Ops:
  1.6 4.7 %collective-permute-start = (bf16[2,6,24,1024]{3,2,1,0:T(8,128)(2,1)S(1)}, bf16[2,6,24,1024]{3,2,1,0:T(8,128)(2,1)}, u32[]{:S(2)}, u32[]{:S(2)}) collective-permute-start(bf16[2,6,24,1024]{3,2,1,0:T(8,128)(2,1)S(1)} %slice.50), channel_id=1, source_target_pairs={{2,0},{4,2},{6,4},{0,6},{3,1},{5,3},{7,5},{1,7},{10,8},{12,10},{14... | collective-permute-start | bytes 1769480 | tf_op jit(solution)/shard_map/ppermute | solution.py:21
  6.2 1.5 collective-permute-start.4
  7.7 34.0 %collective-permute-done.2 = bf16[256,4096]{1,0:T(8,128)(2,1)S(1)} collective-permute-done((bf16[256,4096]{1,0:T(8,128)(2,1)}, bf16[256,4096]{1,0:T(8,128)(2,1)S(1)}, u32[]{:S(2)}, u32[]{:S(2)}) %collective-permute-start.2) | collective-permute-done | bytes 2097184 | tf_op jit(solution)/shard_map/ppermute | solution.py:105
  41.6 1.8 collective-permute-start.3
  46.5 1.6 fusion.18
  48.1 1.4 copy.17
  49.5 1.5 collective-permute-start.1
  54.0 10.6 %collective-permute-done.1 = bf16[2,12,12,1024]{3,0,2,1:T(2,128)(2,1)} collective-permute-done((bf16[2,12,12,1024]{3,0,2,1:T(2,128)(2,1)}, bf16[2,12,12,1024]{3,0,2,1:T(2,128)(2,1)}, u32[]{:S(2)}, u32[]{:S(2)}) %collective-permute-start.1) | collective-permute-done | bytes 589856 | tf_op jit(solution)/shard_map/ppermute | solution.py:21
  67.3 1.4 fusion.14
  68.7 2.7 %collective-permute-done.3 = bf16[256,4096]{1,0:T(8,128)(2,1)} collective-permute-done((bf16[256,4096]{1,0:T(8,128)(2,1)S(1)}, bf16[256,4096]{1,0:T(8,128)(2,1)}, u32[]{:S(2)}, u32[]{:S(2)}) %collective-permute-start.3) | collective-permute-done | bytes 2097184 | tf_op jit(solution)/shard_map/ppermute | solution.py:105
  71.4 3.3 %pad_maximum_fusion = bf16[4,256,4096]{2,1,0:T(8,128)(2,1)S(1)} fusion(bf16[1,256,4096]{2,1,0:T(8,128)(2,1)} %bitcast.7, bf16[1,256,4096]{2,1,0:T(8,128)(2,1)S(1)} %bitcast.60, bf16[1,256,4096]{2,1,0:T(8,128)(2,1)S(1)} %bitcast.61, bf16[1,256,4096]{2,1,0:T(8,128)(2,1)} %bitcast.4), kind=kLoop, calls=%fused_computation.6 | loop fusion | flops 12582912 | bytes 16777216 | tf_op jit(solution)/shard_map/stack | solution.py:108
  74.7 3.8 %fusion.31 = (bf16[4,256,2048]{2,1,0:T(8,128)(2,1)}, bf16[4,256,2048]{2,1,0:T(8,128)(2,1)}) fusion(bf16[4,256,4096]{2,1,0:T(8,128)(2,1)S(1)} %pad_maximum_fusion), kind=kLoop, calls=%fused_computation.55 | loop fusion | bytes 16777216 | tf_op jit(solution)/shard_map/gather | solution.py:110
  78.5 4.9 %gather_fusion = bf16[4,256,2048]{2,1,0:T(8,128)(2,1)} fusion(bf16[4,256,2048]{2,1,0:T(8,128)(2,1)} %get-tuple-element.7, s32[1024]{0:T(1024)S(1)} %pad_clamp_fusion), kind=kCustom, calls=%fused_computation | custom fusion | bytes 8388624 | tf_op jit(solution)/shard_map/gather | solution.py:110
  83.5 5.0 %gather_fusion.1 = bf16[4,256,2048]{2,1,0:T(8,128)(2,1)} fusion(bf16[4,256,2048]{2,1,0:T(8,128)(2,1)} %get-tuple-element.8, s32[1024]{0:T(1024)S(1)} %pad_clamp_fusion), kind=kCustom, calls=%fused_computation.1 | custom fusion | bytes 8388624 | tf_op jit(solution)/shard_map/gather | solution.py:110
  88.5 7.9 %pad_maximum_fusion.1 = bf16[4,256,4096]{2,1,0:T(8,128)(2,1)} fusion(bf16[4,256,2048]{2,1,0:T(8,128)(2,1)} %gather_fusion.1, bf16[4,256,2048]{2,1,0:T(8,128)(2,1)} %gather_fusion), kind=kLoop, calls=%fused_computation.7 | loop fusion | flops 16777216 | bytes 16777216
  96.3 7.0 %fusion.8 = bf16[576,3072]{1,0:T(8,128)(2,1)S(1)} fusion(bf16[576,1024]{1,0:T(8,128)(2,1)} %bitcast.62, bf16[1024,4096]{1,0:T(8,128)(2,1)} %bitcast.51), kind=kOutput, calls=%fused_computation.15 | convolution fusion | flops 3625648128 | bytes 11010048 | tf_op jit(solution)/shard_map/dot_general | solution.py:52
  103.3 3.4 %reshape_reshape.6 = bf16[1,2,2,6,2,12,3072]{6,5,4,3,2,1,0:T(8,128)(2,1)} reshape(bf16[576,3072]{1,0:T(8,128)(2,1)S(1)} %fusion.8) | data formatting | bytes 7077888 | tf_op jit(solution)/shard_map/reshape;reshape | solution.py:34
  106.7 7.8 %copy.19 = bf16[1,2,2,2,6,12,3072]{6,2,1,5,4,3,0:T(2,128)(2,1)} copy(bf16[1,2,2,2,6,12,3072]{6,5,2,4,1,3,0:T(8,128)(2,1)} %bitcast.50) | data formatting | bytes 7077888 | tf_op jit(solution)/shard_map/transpose | solution.py:37
  114.5 7.7 %reshape.98 = bf16[4,144,3072]{2,0,1:T(4,128)(2,1)S(1)} reshape(bf16[1,2,2,2,6,12,3072]{6,2,1,5,4,3,0:T(2,128)(2,1)} %copy.19) | data formatting | bytes 7077888 | tf_op jit(solution)/shard_map/reshape | solution.py:38
  122.1 2.7 %fusion.32 = (bf16[4,144,1024]{2,0,1:T(4,128)(2,1)}, bf16[4,144,1024]{2,0,1:T(4,128)(2,1)}, bf16[4,144,1024]{2,0,1:T(4,128)(2,1)}) fusion(bf16[4,144,3072]{2,0,1:T(4,128)(2,1)S(1)} %reshape.98), kind=kLoop, calls=%fused_computation.56 | loop fusion | bytes 7077888 | tf_op jit(solution)/shard_map/slice | solution.py:59
  124.8 4.1 %copy.22 = bf16[4,144,1024]{1,2,0:T(8,128)(2,1)} copy(bf16[4,144,1024]{2,0,1:T(4,128)(2,1)} %get-tuple-element.10) | data formatting | bytes 2359296 | tf_op jit(solution)/shard_map/slice | solution.py:58
  128.9 2.5 %copy.23 = bf16[4,144,1024]{1,2,0:T(8,128)(2,1)} copy(bf16[4,144,1024]{2,0,1:T(4,128)(2,1)S(1)} %copy-done.1) | data formatting | bytes 2359296 | tf_op jit(solution)/shard_map/slice | solution.py:59
  131.4 2.5 %copy.20 = bf16[4,144,1024]{1,2,0:T(8,128)(2,1)} copy(bf16[4,144,1024]{2,0,1:T(4,128)(2,1)S(1)} %copy-done) | data formatting | bytes 2359296 | tf_op jit(solution)/shard_map/slice | solution.py:60
  133.9 8.8 %fusion.34 = (f32[4,16,144]{2,1,0:T(8,128)S(1)}, f32[4,16,144,144]{2,3,1,0:T(8,128)}) fusion(pred[4,144,144]{1,2,0:T(8,128)(4,1)S(1)} %copy-done.5, bf16[4,144,16,64]{1,3,2,0:T(8,128)(2,1)S(1)} %bitcast.57, bf16[4,144,16,64]{1,3,2,0:T(8,128)(2,1)} %bitcast.58), kind=kOutput, calls=%fused_computation.58 | convolution fusion | flops 175177872 | bytes 7787520 | tf_op jit(solution)/shard_map/sub | solution.py:68
  142.7 6.5 %convert_bitcast_fusion = bf16[4,144,16,64]{1,3,2,0:T(8,128)(2,1)} fusion(bf16[4,144,16,64]{1,3,2,0:T(8,128)(2,1)} %bitcast.59, f32[4,16,144,144]{2,3,1,0:T(8,128)} %get-tuple-element.15, f32[4,16,144]{2,1,0:T(8,128)S(1)} %get-tuple-element.14), kind=kOutput, calls=%fused_computation.25 | convolution fusion | flops 173113344 | bytes 7704576 | tf_op jit(solution)/shard_map/whqk,wkhe->wqhe/dot_general | solution.py:70
  149.3 3.8 %copy.25 = bf16[4,144,16,64]{3,2,0,1:T(8,128)(2,1)S(1)} copy(bf16[4,144,16,64]{1,3,2,0:T(8,128)(2,1)} %convert_bitcast_fusion) | data formatting | bytes 2359296 | tf_op jit(solution)/shard_map/convert_element_type | solution.py:73
  153.0 1.4 reshape_reshape.7
  156.1 2.4 %collective-permute-start.5 = (bf16[2,6,24,1024]{3,2,1,0:T(8,128)(2,1)S(1)}, bf16[2,6,24,1024]{3,2,1,0:T(8,128)(2,1)S(1)}, u32[]{:S(2)}, u32[]{:S(2)}) collective-permute-start(bf16[2,6,24,1024]{3,2,1,0:T(8,128)(2,1)S(1)} %slice.56), channel_id=1, source_target_pairs={{6,0},{0,2},{2,4},{4,6},{7,1},{1,3},{3,5},{5,7},{14,8},{8,10},{10,... | collective-permute-start | bytes 1769480 | tf_op jit(solution)/shard_map/ppermute | solution.py:21
  159.6 14.4 %collective-permute-done.5 = bf16[2,6,24,1024]{3,2,1,0:T(8,128)(2,1)S(1)} collective-permute-done((bf16[2,6,24,1024]{3,2,1,0:T(8,128)(2,1)S(1)}, bf16[2,6,24,1024]{3,2,1,0:T(8,128)(2,1)S(1)}, u32[]{:S(2)}, u32[]{:S(2)}) %collective-permute-start.5) | collective-permute-done | bytes 589856 | tf_op jit(solution)/shard_map/ppermute | solution.py:21
  175.1 2.1 %collective-permute-start.6 = (bf16[2,12,12,1024]{3,0,2,1:T(2,128)(2,1)S(1)}, bf16[2,12,12,1024]{3,0,2,1:T(2,128)(2,1)S(1)}, u32[]{:S(2)}, u32[]{:S(2)}) collective-permute-start(bf16[2,12,12,1024]{3,0,2,1:T(2,128)(2,1)S(1)} %copy.29), channel_id=1, source_target_pairs={{1,0},{0,1},{3,2},{2,3},{5,4},{4,5},{7,6},{6,7},{9,8},{8,9},{11,10... | collective-permute-start | bytes 1769480 | tf_op jit(solution)/shard_map/ppermute | solution.py:21
  178.4 12.5 %collective-permute-done.6 = bf16[2,12,12,1024]{3,0,2,1:T(2,128)(2,1)S(1)} collective-permute-done((bf16[2,12,12,1024]{3,0,2,1:T(2,128)(2,1)S(1)}, bf16[2,12,12,1024]{3,0,2,1:T(2,128)(2,1)S(1)}, u32[]{:S(2)}, u32[]{:S(2)}) %collective-permute-start.6) | collective-permute-done | bytes 589856 | tf_op jit(solution)/shard_map/ppermute | solution.py:21
  191.1 4.3 %fusion.16 = bf16[1,2,12,24,1024]{4,3,2,1,0:T(8,128)(2,1)} fusion(bf16[1024,4096]{1,0:T(8,128)(2,1)} %bitcast.52, s32[]{:T(128)S(6)} %select_n.46, bf16[2,12,12,1024]{3,2,1,0:T(8,128)(2,1)S(1)} %copy.30, bf16[2,12,24,1024]{3,2,1,0:T(8,128)(2,1)S(1)} %fusion.17, bf16[1,2,12,24,1024]{4,3,2,1,0:T(8,128)(2,1)S(1)} %copy-done.2), kind=kOutput, calls=%fused_computation.34 | convolution fusion | flops 1212088320 | bytes 6225924 | tf_op jit(solution)/shard_map/dot_general | solution.py:116
  (38 shorter events, 9.6 us)
Async XLA Ops:
  0.0 41.6 %collective-permute-start.2 = (bf16[256,4096]{1,0:T(8,128)(2,1)}, bf16[256,4096]{1,0:T(8,128)(2,1)S(1)}, u32[]{:S(2)}, u32[]{:S(2)}) collective-permute-start(bf16[256,4096]{1,0:T(8,128)(2,1)} %param.5), channel_id=1, source_target_pairs={{0,8},{8,16},{16,24},{24,0},{1,9},{9,17},{17,25},{25,1},{2,10},{10... | collective-permute-start | bytes 6291464 | tf_op jit(solution)/shard_map/ppermute | solution.py:105
  1.6 44.9 %collective-permute-start = (bf16[2,6,24,1024]{3,2,1,0:T(8,128)(2,1)S(1)}, bf16[2,6,24,1024]{3,2,1,0:T(8,128)(2,1)}, u32[]{:S(2)}, u32[]{:S(2)}) collective-permute-start(bf16[2,6,24,1024]{3,2,1,0:T(8,128)(2,1)S(1)} %slice.50), channel_id=1, source_target_pairs={{2,0},{4,2},{6,4},{0,6},{3,1},{5,3},{7,5},{1,7},{10,8},{12,10},{14... | collective-permute-start | bytes 1769480 | tf_op jit(solution)/shard_map/ppermute | solution.py:21
  6.2 62.5 %collective-permute-start.4 = (bf16[256,4096]{1,0:T(8,128)(2,1)}, bf16[256,4096]{1,0:T(8,128)(2,1)}, u32[]{:S(2)}, u32[]{:S(2)}) collective-permute-start(bf16[256,4096]{1,0:T(8,128)(2,1)} %param.5), channel_id=1, source_target_pairs={{8,0},{16,8},{24,16},{0,24},{9,1},{17,9},{25,17},{1,25},{10,2},{18... | collective-permute-start | bytes 6291464 | tf_op jit(solution)/shard_map/ppermute | solution.py:107
  41.6 29.7 %collective-permute-start.3 = (bf16[256,4096]{1,0:T(8,128)(2,1)S(1)}, bf16[256,4096]{1,0:T(8,128)(2,1)}, u32[]{:S(2)}, u32[]{:S(2)}) collective-permute-start(bf16[256,4096]{1,0:T(8,128)(2,1)S(1)} %collective-permute-done.2), channel_id=1, source_target_pairs={{0,8},{8,16},{16,24},{24,0},{1,9},{9,17},{17,25},{25,1},{2,10},{10... | collective-permute-start | bytes 6291464 | tf_op jit(solution)/shard_map/ppermute | solution.py:105
  46.4 5.9 %copy-start.6 = (s32[2,12,24]{2,0,1:T(2,128)S(1)}, s32[2,12,24]{2,0,1:T(2,128)}, u32[]{:S(2)}) copy-start(s32[2,12,24]{2,0,1:T(2,128)} %param.6) | copy-start | bytes 6916
  49.5 15.1 %collective-permute-start.1 = (bf16[2,12,12,1024]{3,0,2,1:T(2,128)(2,1)}, bf16[2,12,12,1024]{3,0,2,1:T(2,128)(2,1)}, u32[]{:S(2)}, u32[]{:S(2)}) collective-permute-start(bf16[2,12,12,1024]{3,0,2,1:T(2,128)(2,1)} %copy.17), channel_id=1, source_target_pairs={{1,0},{0,1},{3,2},{2,3},{5,4},{4,5},{7,6},{6,7},{9,8},{8,9},{11,10... | collective-permute-start | bytes 1769480 | tf_op jit(solution)/shard_map/ppermute | solution.py:21
  66.8 4.5 %copy-start.4 = (bf16[256,4096]{1,0:T(8,128)(2,1)S(1)}, bf16[256,4096]{1,0:T(8,128)(2,1)}, u32[]{:S(2)}) copy-start(bf16[256,4096]{1,0:T(8,128)(2,1)} %param.5) | copy-start | bytes 6291460
  124.8 4.1 %copy-start.1 = (bf16[4,144,1024]{2,0,1:T(4,128)(2,1)S(1)}, bf16[4,144,1024]{2,0,1:T(4,128)(2,1)}, u32[]{:S(2)}) copy-start(bf16[4,144,1024]{2,0,1:T(4,128)(2,1)} %get-tuple-element.9) | copy-start | bytes 3538948
  128.9 2.5 %copy-start = (bf16[4,144,1024]{2,0,1:T(4,128)(2,1)S(1)}, bf16[4,144,1024]{2,0,1:T(4,128)(2,1)}, u32[]{:S(2)}) copy-start(bf16[4,144,1024]{2,0,1:T(4,128)(2,1)} %get-tuple-element.11) | copy-start | bytes 3538948
  131.4 2.5 %copy-start.3 = (bf16[4,144,1024]{1,2,0:T(8,128)(2,1)S(1)}, bf16[4,144,1024]{1,2,0:T(8,128)(2,1)}, u32[]{:S(2)}) copy-start(bf16[4,144,1024]{1,2,0:T(8,128)(2,1)} %copy.22) | copy-start | bytes 3538948
  131.4 2.5 %copy-start.5 = (pred[4,144,144]{1,2,0:T(8,128)(4,1)S(1)}, pred[4,144,144]{1,2,0:T(8,128)(4,1)}, u32[]{:S(2)}) copy-start(pred[4,144,144]{1,2,0:T(8,128)(4,1)} %broadcast_compare_fusion) | copy-start | bytes 248836
  156.1 17.9 %collective-permute-start.5 = (bf16[2,6,24,1024]{3,2,1,0:T(8,128)(2,1)S(1)}, bf16[2,6,24,1024]{3,2,1,0:T(8,128)(2,1)S(1)}, u32[]{:S(2)}, u32[]{:S(2)}) collective-permute-start(bf16[2,6,24,1024]{3,2,1,0:T(8,128)(2,1)S(1)} %slice.56), channel_id=1, source_target_pairs={{6,0},{0,2},{2,4},{4,6},{7,1},{1,3},{3,5},{5,7},{14,8},{8,10},{10,... | collective-permute-start | bytes 1769480 | tf_op jit(solution)/shard_map/ppermute | solution.py:21
  174.3 16.9 %copy-start.2 = (bf16[1,2,12,24,1024]{4,3,2,1,0:T(8,128)(2,1)S(1)}, bf16[1,2,12,24,1024]{4,3,2,1,0:T(8,128)(2,1)}, u32[]{:S(2)}) copy-start(bf16[1,2,12,24,1024]{4,3,2,1,0:T(8,128)(2,1)} %param.4) | copy-start | bytes 3538948
  175.1 15.8 %collective-permute-start.6 = (bf16[2,12,12,1024]{3,0,2,1:T(2,128)(2,1)S(1)}, bf16[2,12,12,1024]{3,0,2,1:T(2,128)(2,1)S(1)}, u32[]{:S(2)}, u32[]{:S(2)}) collective-permute-start(bf16[2,12,12,1024]{3,0,2,1:T(2,128)(2,1)S(1)} %copy.29), channel_id=1, source_target_pairs={{1,0},{0,1},{3,2},{2,3},{5,4},{4,5},{7,6},{6,7},{9,8},{8,9},{11,10... | collective-permute-start | bytes 1769480 | tf_op jit(solution)/shard_map/ppermute | solution.py:21
